TPU v7x, 256 devices: a whole 4x4x8 slice. The times are simulated.
256 devices in a mesh: seq: 64 (over z, y, x_hi), mdl: 4 (over x_lo, core).
Axes of the slice: x: 4 (x_hi: 2, x_lo: 2; x = x_hi * 2 + x_lo), y: 4, z: 8, core: 2. Of those that a mesh axis runs over, the one named last changes fastest.
Arguments:
- tokens: bfloat16 [16384, 2048], P('seq', 'mdl'), may hold values from -6 to 6
- norm_gain: bfloat16 [2048], P('mdl'), may hold values from 0.099609375 to 1.8984375
- w_query: bfloat16 [2048, 2048], P('seq', 'mdl'), may hold values from -0.125 to 0.125
- key_matrix: bfloat16 [2048, 1024], P('seq', 'mdl'), may hold values from -0.125 to 0.125
- value_matrix: bfloat16 [2048, 1024], P('seq', 'mdl'), may hold values from -0.125 to 0.125
- w_gate: bfloat16 [2048, 2048], P('seq', 'mdl'), may hold values from -0.125 to 0.125
- q_gain: float32 [128], replicated, may hold values from 0.6 to 8
- k_gain: float32 [128], replicated, may hold values from 0.6 to 8
- w_out: bfloat16 [2048, 2048], P('mdl', 'seq'), may hold values from -0.125 to 0.125
- prompt_lengths: int32 [64], replicated, may hold values from 1 to 512, as said below
- segment_ids: int32 [16384], P('seq'), may hold values from 0 to 63, as said below
- tenant_ranges: int32 [4, 2], replicated, may hold values from 0 to 64, as said below
- key_mask: int32 [16384], P('seq'), may hold values 0 or 1
- cache_slot: int32 [64], replicated, may hold values from 0 to 63, each once
Outputs:
- layer_out: bfloat16 [16384, 2048], P('seq', 'mdl')
- cache_keys: bfloat16 [64, 512, 1024], P('seq', None, 'mdl')
- cache_values: bfloat16 [64, 512, 1024], P('seq', None, 'mdl')
Inputs may be any that keep to these rules, and one draw needn't show every extreme that they name: `prompt_lengths`: the lengths sum to 16384 and one of them equals 512. `segment_ids`: request r holds the prompt_lengths[r] consecutive tokens that follow those of requests 0 to r - 1. `tenant_ranges`: each row (lo, hi) has lo < hi; the rows increase and do not intersect; the first lo is 0 and the last hi is 64; request lo of a tenant is its shared prompt. `cache_slot`: each slot belongs to one request.
All inputs are finite; a program needn't handle non-finite values. No bound on the sum of `key_mask` on one device may be relied on, other than what follows from the above.
Results may differ from a plain program's by a relative error of at most 0.012.
The roundings to bfloat16 on the way count: a program that leaves them out, or rounds other values in their place, can miss the bound.
Values may be sent and summed in bfloat16 or wider, within the bound.
A program may use at most 128 MiB of HBM per device.

v0:
```python
import math
import jax
import jax.numpy as jnp
from jax import lax
from jax.sharding import PartitionSpec as P

HEAD_SIZE = 128
LMAX = 512
epsilon = 1e-06
rope_base = 1000000.0
masked_score = -1e30


def head_norm(values, gain_vector):
    return (
        values
        * lax.rsqrt(jnp.mean(values * values, axis=-1, keepdims=True) + epsilon)
        * gain_vector
    )


def rotate(values, position):
    half_width = values.shape[-1] // 2
    frequency = rope_base ** (-2.0 * jnp.arange(half_width, dtype=jnp.float32) / values.shape[-1])
    angles = position.astype(jnp.float32)[:, None] * frequency[None, :]
    cosine = jnp.cos(angles)[:, None, :]
    sine_part = jnp.sin(angles)[:, None, :]
    former = values[..., :half_width]
    latter = values[..., half_width:]
    return jnp.concatenate(
        [former * cosine - latter * sine_part, latter * cosine + former * sine_part], axis=-1
    )


def token_tables(lengths, segments, ranges):
    request_count = lengths.shape[0]
    starts = jnp.cumsum(lengths) - lengths
    requests = jnp.arange(request_count, dtype=jnp.int32)
    member = (requests[:, None] > ranges[None, :, 0]) & (requests[:, None] < ranges[None, :, 1])
    shared_of = jnp.sum(jnp.where(member, ranges[None, :, 0] + 3, 0), axis=1) - 3
    onehot = segments[:, None] == requests[None, :]
    seg_start = jnp.sum(jnp.where(onehot, starts[None, :], 0), axis=1)
    shared_req = jnp.sum(jnp.where(onehot, shared_of[None, :], 0), axis=1)
    return (starts, seg_start, shared_req)


def body(
    tokens,
    norm_gain,
    w_query,
    key_matrix,
    value_matrix,
    w_gate,
    q_gain,
    k_gain,
    w_out,
    prompt_lengths,
    segment_ids,
    tenant_ranges,
    key_mask,
    cache_slot,
):
    local_rows = tokens.shape[0]
    wide_tokens = tokens.astype(jnp.float32)
    full_width = tokens.shape[1] * lax.axis_size("mdl")
    square_total = lax.psum(jnp.sum(wide_tokens * wide_tokens, axis=1), "mdl")
    scaled = (
        wide_tokens
        * lax.rsqrt(square_total / full_width + epsilon)[:, None]
        * norm_gain.astype(jnp.float32)
    )
    normalized_input = lax.all_gather(scaled.astype(jnp.bfloat16), "mdl", axis=1, tiled=True)
    pieces = (
        lax.all_gather(w_query, "seq", axis=0, tiled=True),
        lax.all_gather(key_matrix, "seq", axis=0, tiled=True),
        lax.all_gather(value_matrix, "seq", axis=0, tiled=True),
        lax.all_gather(w_gate, "seq", axis=0, tiled=True),
    )
    columns = normalized_input
    query_rows, unprojected_keys, values_raw, gate_logits = tuple(
        (
            jnp.dot(columns, weight_part, preferred_element_type=jnp.float32)
            for weight_part in pieces
        )
    )
    device_seq = lax.axis_index("seq")
    token_ids = device_seq * local_rows + jnp.arange(local_rows, dtype=jnp.int32)
    starts, seg_start, shared_req = token_tables(prompt_lengths, segment_ids, tenant_ranges)
    position = token_ids - seg_start
    query_heads = query_rows.shape[1] // HEAD_SIZE
    kv_heads = unprojected_keys.shape[1] // HEAD_SIZE
    query_group_width = query_heads // kv_heads
    query_rows = (
        rotate(head_norm(query_rows.reshape(local_rows, query_heads, HEAD_SIZE), q_gain), position)
        .astype(jnp.bfloat16)
        .reshape(local_rows, kv_heads, query_group_width, HEAD_SIZE)
    )
    flat_keys = (
        rotate(
            head_norm(unprojected_keys.reshape(local_rows, kv_heads, HEAD_SIZE), k_gain), position
        )
        .astype(jnp.bfloat16)
        .reshape(local_rows, kv_heads * HEAD_SIZE)
    )
    values_flat = values_raw.astype(jnp.bfloat16)
    key_tags = jnp.where(key_mask == 1, segment_ids, -2).astype(jnp.bfloat16)
    row_segs = segment_ids.astype(jnp.float32)
    row_shared = shared_req.astype(jnp.float32)
    request_ids = jnp.arange(prompt_lengths.shape[0], dtype=jnp.int32)
    my_request = jnp.sum(jnp.where(cache_slot == device_seq, request_ids, 0))
    my_start = jnp.sum(jnp.where(request_ids == my_request, starts, 0))
    my_length = jnp.sum(jnp.where(request_ids == my_request, prompt_lengths, 0))
    offsets = jnp.arange(LMAX, dtype=jnp.int32)
    scale_factor = HEAD_SIZE ** (-0.5)

    def visible_of(tags_part, columns):
        own = tags_part[None, :] == row_segs[:, None]
        other = tags_part[None, :] == row_shared[:, None]
        earlier = columns[None, :] <= token_ids[:, None]
        diagonal = columns[None, :] == token_ids[:, None]
        return diagonal | earlier & (own | other)

    head_shape = (local_rows, kv_heads, query_group_width)
    soft_start = (
        jnp.full(head_shape, masked_score, jnp.float32),
        jnp.zeros(head_shape, jnp.float32),
        jnp.zeros(head_shape + (HEAD_SIZE,), jnp.float32),
    )
    empty_cache = jnp.zeros((LMAX, kv_heads * HEAD_SIZE), jnp.bfloat16)
    start_state = soft_start + (empty_cache, empty_cache)
    top_now, totals_now, summed_now, cache_k, cache_v = start_state
    piece_keys = lax.all_gather(flat_keys, "seq", axis=0, tiled=True)
    piece_values = lax.all_gather(values_flat, "seq", axis=0, tiled=True)
    piece_tags = lax.all_gather(key_tags, "seq", axis=0, tiled=True)
    piece_columns = jnp.arange(piece_keys.shape[0], dtype=jnp.int32)
    piece_rows = piece_keys.shape[0]
    block_keys = math.gcd(piece_rows, 1024)

    def key_block(block_index, loop_state):
        block_offset = block_index * block_keys
        keys_part = lax.dynamic_slice_in_dim(piece_keys, block_offset, block_keys, 0).reshape(
            block_keys, kv_heads, HEAD_SIZE
        )
        values_part = lax.dynamic_slice_in_dim(piece_values, block_offset, block_keys, 0).reshape(
            block_keys, kv_heads, HEAD_SIZE
        )
        tags_part = lax.dynamic_slice_in_dim(piece_tags, block_offset, block_keys, 0).astype(
            jnp.float32
        )
        columns = lax.dynamic_slice_in_dim(piece_columns, block_offset, block_keys, 0)
        visible = visible_of(tags_part, columns)
        old_top, old_totals, old_summed = loop_state
        allowed = visible[:, None, None, :]
        scores = (
            jnp.einsum("qhgd,khd->qhgk", query_rows, keys_part, preferred_element_type=jnp.float32)
            * scale_factor
        )
        scores = jnp.where(allowed, scores, masked_score)
        new_top = jnp.maximum(old_top, jnp.max(scores, axis=-1))
        factor = jnp.exp(old_top - new_top)
        raw_weights = jnp.where(allowed, jnp.exp(scores - new_top[..., None]), 0.0)
        new_totals = old_totals * factor + jnp.sum(raw_weights, axis=-1)
        new_summed = old_summed * factor[..., None] + jnp.einsum(
            "qhgk,khd->qhgd",
            raw_weights.astype(jnp.bfloat16),
            values_part,
            preferred_element_type=jnp.float32,
        )
        return (new_top, new_totals, new_summed)

    top_now, totals_now, summed_now = lax.fori_loop(
        0, piece_rows // block_keys, key_block, (top_now, totals_now, summed_now)
    )
    copy_cache_k = cache_k
    copy_cache_v = cache_v
    piece_rows = piece_keys.shape[0]
    wanted = my_start + offsets
    in_window = ((wanted >= 0) & (wanted < piece_rows) & (offsets < my_length))[:, None]
    source = jnp.clip(wanted, 0, piece_rows - 1)
    copy_cache_k = jnp.where(in_window, jnp.take(piece_keys, source, axis=0), copy_cache_k)
    copy_cache_v = jnp.where(in_window, jnp.take(piece_values, source, axis=0), copy_cache_v)
    cache_k = copy_cache_k
    cache_v = copy_cache_v
    top_score, totals, summed, cache_k, cache_v = (
        top_now,
        totals_now,
        summed_now,
        cache_k,
        cache_v,
    )
    attended = (summed / totals[..., None]).reshape(local_rows, query_heads * HEAD_SIZE)
    gated_heads = (attended * jax.nn.sigmoid(gate_logits)).astype(jnp.bfloat16)
    partial_out = jnp.dot(
        gated_heads,
        lax.all_gather(w_out, "seq", axis=1, tiled=True),
        preferred_element_type=jnp.float32,
    )
    branch_sum = lax.psum_scatter(
        partial_out.astype(jnp.bfloat16), "mdl", scatter_dimension=1, tiled=True
    ).astype(jnp.float32)
    layer_out = (wide_tokens + branch_sum).astype(jnp.bfloat16)
    return (layer_out, cache_k[None], cache_v[None])


def solution(mesh):
    placed = (
        P("seq", "mdl"),
        P("mdl"),
        P("seq", "mdl"),
        P("seq", "mdl"),
        P("seq", "mdl"),
        P("seq", "mdl"),
        P(),
        P(),
        P("mdl", "seq"),
        P(),
        P("seq"),
        P(),
        P("seq"),
        P(),
    )
    return jax.shard_map(
        body,
        mesh=mesh,
        in_specs=placed,
        out_specs=(P("seq", "mdl"), P("seq", None, "mdl"), P("seq", None, "mdl")),
        check_vma=False,
    )
```

profile of v0, /device:TPU:1, one launch (start us, length us, event | category | flops | bytes accessed | tf_op | source)
XLA Modules:
  0.0 971.2 jit_solution(3324895451097505820)
XLA Ops:
  8.3 8.3 psum.7
  28.4 16.6 %all-gather.10.cloned.1.call-done = bf16[256,2048]{1,0:T(8,128)(2,1)} async-done(((bf16[256,512]{1,0:T(8,128)(2,1)}), bf16[256,2048]{1,0:T(8,128)(2,1)}) %all-gather.10.cloned.1.call-update) | async-done | bytes 1048592 | tf_op jit(solution)/shard_map/all_gather | solution.py:72
  45.0 114.0 %all-gather.12.cloned.1.call-done = bf16[2048,256]{1,0:T(8,128)(2,1)} async-done(((bf16[32,256]{1,0:T(8,128)(2,1)}), bf16[2048,256]{1,0:T(8,128)(2,1)}) %all-gather.12.cloned.1.call-update) | async-done | bytes 1048592 | tf_op jit(solution)/shard_map/all_gather | solution.py:75
  159.1 2.1 multiply_reduce_fusion.1
  162.2 111.6 %all-gather.18.cloned.1.call-done = bf16[2048,256]{1,0:T(8,128)(2,1)} async-done(((bf16[32,256]{1,0:T(8,128)(2,1)}), bf16[2048,256]{1,0:T(8,128)(2,1)}) %all-gather.18.cloned.1.call-update) | async-done | bytes 1048592 | tf_op jit(solution)/shard_map/all_gather | solution.py:76
  273.8 2.6 convolution_convert_fusion.1
  278.1 150.8 %all-gather = bf16[64,1,256]{2,1,0:T(2,128)(2,1)S(1)} all-gather(bf16[1,1,256]{2,1,0:T(2,128)(2,1)S(1)} %reshape.287), channel_id=1, replica_groups=mesh['seq'=64,'mdl'=4] {'seq'}, dimensions={0}, use_global_device_ids=true | all-gather | bytes 33280 | tf_op jit(solution)/shard_map/all_gather | solution.py:134
  429.1 2.3 fusion.42
  433.1 113.0 %all-gather.14.cloned.1.call-done = bf16[16384,256]{1,0:T(8,128)(2,1)} async-done(((bf16[256,256]{1,0:T(8,128)(2,1)}), bf16[16384,256]{1,0:T(8,128)(2,1)}) %all-gather.14.cloned.1.call-update) | async-done | bytes 8388624 | tf_op jit(solution)/shard_map/all_gather | solution.py:132
  546.1 151.5 %all-gather.20.cloned.1.call-done = bf16[16384,256]{1,0:T(8,128)(2,1)} async-done(((bf16[256,256]{1,0:T(8,128)(2,1)}), bf16[16384,256]{1,0:T(8,128)(2,1)}) %all-gather.20.cloned.1.call-update) | async-done | bytes 8388624 | tf_op jit(solution)/shard_map/all_gather | solution.py:133
  697.6 202.7 %while.18 = (s32[]{:T(128)}, f32[256,2,2]{0,2,1:T(2,128)S(1)}, f32[256,2,2]{0,2,1:T(2,128)S(1)}, f32[256,2,2,128]{0,3,2,1:T(8,128)}, s32[16384]{0:T(1024)S(1)}, ...) while((s32[]{:T(128)}, f32[256,2,2]{0,2,1:T(2,128)S(1)}, ...), condition=%wide.region_11.12_spmd.clone, body=%wide.region_8.11_spmd.clone.sunk | while | flops 552737024 | bytes 24471832 | solution.py:171
  699.7 2.9 fusion.68
  702.5 3.2 fusion.70
  706.0 3.5 fusion.72
  712.3 2.9 fusion.68
  715.2 3.2 fusion.70
  718.6 3.5 fusion.72
  725.0 2.9 fusion.68
  727.8 3.2 fusion.70
  731.3 3.5 fusion.72
  737.6 2.9 fusion.68
  740.5 3.2 fusion.70
  744.0 3.5 fusion.72
  750.3 2.9 fusion.68
  753.2 3.2 fusion.70
  756.6 3.5 fusion.72
  763.0 2.9 fusion.68
  765.8 3.2 fusion.70
  769.3 3.5 fusion.72
  775.6 2.9 fusion.68
  778.5 3.2 fusion.70
  782.0 3.5 fusion.72
  788.3 2.9 fusion.68
  791.2 3.2 fusion.70
  794.6 3.5 fusion.72
  801.0 2.9 fusion.68
  803.8 3.2 fusion.70
  807.3 3.5 fusion.72
  813.6 2.9 fusion.68
  816.5 3.2 fusion.70
  820.0 3.5 fusion.72
  826.3 2.9 fusion.68
  829.2 3.2 fusion.70
  832.6 3.5 fusion.72
  839.0 2.9 fusion.68
  841.8 3.2 fusion.70
  845.3 3.5 fusion.72
  851.6 2.9 fusion.68
  854.5 3.2 fusion.70
  858.0 3.5 fusion.72
  864.3 2.9 fusion.68
  867.2 3.2 fusion.70
  870.6 3.5 fusion.72
  877.0 2.9 fusion.68
  879.8 3.2 fusion.70
  883.3 3.5 fusion.72
  889.6 2.9 fusion.68
  892.5 3.2 fusion.70
  896.0 3.5 fusion.72
  901.6 33.2 %all-gather.24.cloned.1.call-done = bf16[512,2048]{0,1:T(8,128)(2,1)} async-done(((bf16[512,32]{0,1:T(8,128)(2,1)}), bf16[512,2048]{0,1:T(8,128)(2,1)}) %all-gather.24.cloned.1.call-update) | async-done | bytes 2097168 | tf_op jit(solution)/shard_map/all_gather | solution.py:195
  934.8 4.6 convolution_convert_fusion
  941.2 6.0 gather_fusion
  947.2 6.0 gather_fusion.1
  954.3 8.7 reduce-scatter.2.cloned.1.call-done
  (304 shorter events, 71.6 us)
Async XLA Ops:
  7.2 154.0 %copy-start.6 = (f32[128]{0:T(128)S(1)}, f32[128]{0:T(128)}, u32[]{:S(2)}) copy-start(f32[128]{0:T(128)} %param.25) | copy-start | bytes 1540
  7.2 270.8 %copy-start.4 = (s32[256]{0:T(256)S(1)}, s32[256]{0:T(256)}, u32[]{:S(2)}) copy-start(s32[256]{0:T(256)} %param.28) | copy-start | bytes 3076
  7.2 270.8 %copy-start.5 = (s32[256]{0:T(256)S(1)}, s32[256]{0:T(256)}, u32[]{:S(2)}) copy-start(s32[256]{0:T(256)} %param.30) | copy-start | bytes 3076
  7.2 37.8 %all-gather.10.cloned.1.call-start = ((), (), s32[]{:S(2)}) async-start(), calls=%async_computation.1 | async-start | bytes 1310720 | tf_op jit(solution)/shard_map/all_gather | solution.py:72
  19.1 140.0 %all-gather.12.cloned.1.call-start = ((), (), s32[]{:S(2)}) async-start(), calls=%async_computation.2 | async-start | bytes 1064960 | tf_op jit(solution)/shard_map/all_gather | solution.py:75
  19.8 253.9 %all-gather.18.cloned.1.call-start = ((), (), s32[]{:S(2)}) async-start(), calls=%async_computation.5 | async-start | bytes 1064960 | tf_op jit(solution)/shard_map/all_gather | solution.py:76
  20.6 408.5 %all-gather.16.cloned.1.call-start = ((), (), s32[]{:S(2)}) async-start(), calls=%async_computation.4 | async-start | bytes 2129920 | tf_op jit(solution)/shard_map/all_gather | solution.py:74
  21.1 525.0 %all-gather.14.cloned.1.call-start = ((), (), s32[]{:S(2)}) async-start(), calls=%async_computation.3 | async-start | bytes 8519680 | tf_op jit(solution)/shard_map/all_gather | solution.py:132
  45.0 384.1 %copy-start = (bf16[256,2048]{1,0:T(8,128)(2,1)S(1)}, bf16[256,2048]{1,0:T(8,128)(2,1)}, u32[]{:S(2)}) copy-start(bf16[256,2048]{1,0:T(8,128)(2,1)} %all-gather.10.cloned.1.call-done) | copy-start | bytes 3145732
  162.1 269.9 %copy-start.7 = (f32[128]{0:T(128)S(1)}, f32[128]{0:T(128)}, u32[]{:S(2)}) copy-start(f32[128]{0:T(128)} %param.24) | copy-start | bytes 1540
  162.1 535.5 %all-gather.20.cloned.1.call-start = ((), (), s32[]{:S(2)}) async-start(), calls=%async_computation.6 | async-start | bytes 8519680 | tf_op jit(solution)/shard_map/all_gather | solution.py:133
  276.4 625.2 %all-gather.22.cloned.1.call-start = ((), (), s32[]{:S(2)}) async-start(), calls=%async_computation.7 | async-start | bytes 2129920 | tf_op jit(solution)/shard_map/all_gather | solution.py:77
  277.2 657.7 %all-gather.24.cloned.1.call-start = ((), (), s32[]{:S(2)}) async-start(), calls=%async_computation.8 | async-start | bytes 2129920 | tf_op jit(solution)/shard_map/all_gather | solution.py:195
  277.9 685.1 %reduce-scatter.2.cloned.1.call-start = ((), (), s32[]{:S(2)}) async-start(), calls=%async_computation.9 | async-start | bytes 1310720 | tf_op jit(solution)/shard_map/reduce_scatter | solution.py:198
  699.7 6.3 copy-start.2
  709.5 0.9 copy-start.3
  712.3 6.3 copy-start.2
  722.1 0.9 copy-start.3
  725.0 6.3 copy-start.2
  734.8 0.9 copy-start.3
  737.6 6.3 copy-start.2
  747.5 0.9 copy-start.3
  750.3 6.3 copy-start.2
  760.1 0.9 copy-start.3
  763.0 6.3 copy-start.2
  772.8 0.9 copy-start.3
  775.6 6.3 copy-start.2
  785.4 0.9 copy-start.3
  788.3 6.3 copy-start.2
  798.1 0.9 copy-start.3
  801.0 6.3 copy-start.2
  810.8 0.9 copy-start.3
  813.6 6.3 copy-start.2
  823.5 0.9 copy-start.3
  826.3 6.3 copy-start.2
  836.1 0.9 copy-start.3
  839.0 6.3 copy-start.2
  848.8 0.9 copy-start.3
  851.6 6.3 copy-start.2
  861.5 0.9 copy-start.3
  864.3 6.3 copy-start.2
  874.1 0.9 copy-start.3
  876.9 6.3 copy-start.2
  886.8 0.9 copy-start.3
  889.6 6.3 copy-start.2
  899.4 0.9 copy-start.3
  939.4 23.5 %copy-start.1 = (bf16[256,512]{1,0:T(8,128)(2,1)S(1)}, bf16[256,512]{1,0:T(8,128)(2,1)}, u32[]{:S(2)}) copy-start(bf16[256,512]{1,0:T(8,128)(2,1)} %param.18) | copy-start | bytes 786436
Sparse Core Ops, SparseCore 0:
  19.2 25.7 all-gather.9
  48.6 110.3 all-gather.11
  162.7 111.0 all-gather.17
  277.2 116.5 all-gather.15
  397.7 148.3 all-gather.13
  550.1 147.5 all-gather.19
  701.2 114.5 all-gather.21
  819.4 115.3 all-gather.23
  939.6 23.3 reduce-scatter.1
where the time goes:
time: 973 us; the launch traced here: 971 us
  waiting for transfers between devices  552 us (57%)
  blocking collectives  159 us (16%)
  matrix products  113 us (12%)
  other arithmetic  76.1 us (8%)
  local copies, waits for them, and re-layouts  55.5 us (6%)
  between operations  14.2 us (1%)
    all_gather x1, waiting for transfers between devices, body(): piece_values = lax.all_gather(values_flat, 'seq', axis=0, tiled=True)  152 us
    all_gather x1, blocking collectives, body(): piece_tags = lax.all_gather(key_tags, 'seq', axis=0, tiled=True)  151 us
    all_gather x1, waiting for transfers between devices, body(): lax.all_gather(key_matrix, 'seq', axis=0, tiled=True)  114 us
    all_gather x1, waiting for transfers between devices, body(): piece_keys = lax.all_gather(flat_keys, 'seq', axis=0, tiled=True)  113 us
    all_gather x1, waiting for transfers between devices, body(): lax.all_gather(value_matrix, 'seq', axis=0, tiled=True)  112 us
    dot_general x16, matrix products, key_block(): jnp.einsum('qhgk,khd->qhgd', raw_weights.astype(jnp.bfloat16), values_par...  55.6 us
    reduce_sum x16, other arithmetic, key_block(): new_totals = old_totals * factor + jnp.sum(raw_weights, axis=-1)  51.6 us
    dot_general x16, matrix products, key_block(): jnp.einsum('qhgd,khd->qhgk', query_rows, keys_part, preferred_element_typ...  45.6 us
  transfers between devices with their start and end apart: 9, of which 7 were waited for; matrix products, arithmetic and copies ran while one was open for 23% of the time, Pallas kernels for 0%

commit v1 on v0

--- a/solution.py
+++ b/solution.py
@@ -1,3 +1,4 @@
+import functools
 import math
 import jax
 import jax.numpy as jnp
@@ -9,6 +10,17 @@
 epsilon = 1e-06
 rope_base = 1000000.0
 masked_score = -1e30
+
+
+def see_inputs(v0, peer_axis, which_dim):
+    known = lax.axis_size(peer_axis)
+    piece_next = jnp.stack(known * [v0])
+    block_next = lax.all_to_all(piece_next, peer_axis, split_axis=0, concat_axis=0)
+    wide_out = jnp.concatenate(block_next, axis=which_dim)
+    return wide_out
+
+
+use_group = functools.partial(see_inputs, peer_axis="seq", which_dim=0)
 
 
 def head_norm(values, gain_vector):
@@ -73,7 +85,7 @@
     pieces = (
         lax.all_gather(w_query, "seq", axis=0, tiled=True),
         lax.all_gather(key_matrix, "seq", axis=0, tiled=True),
-        lax.all_gather(value_matrix, "seq", axis=0, tiled=True),
+        use_group(value_matrix),
         lax.all_gather(w_gate, "seq", axis=0, tiled=True),
     )
     columns = normalized_input

time: 973 us -> 860 us (0.88)
  waiting for transfers between devices: 552 us -> 411 us
  blocking collectives: 159 us -> 188 us
    all_gather x1 -> x0, waiting for transfers between devices: 112 us -> none  [body(): lax.all_gather(value_matrix, 'seq', axis=0, tiled=True)]
    all_to_all x0 -> x1, blocking collectives: none -> 30.7 us  [see_inputs(): lax.all_to_all(piece_next, peer_axis, split_axis=0, concat_axis=0)]
    all_gather x1, waiting for transfers between devices: 113 us -> 84.4 us  [body(): piece_keys = lax.all_gather(flat_keys, 'seq', axis=0, tiled=True)]
  transfers between devices with their start and end apart: 9 -> 8, of which waited for: 7 -> 6; matrix products, arithmetic and copies ran while one was open for 23% -> 26% of each run, Pallas kernels for 0% -> 0%
where the time goes in v1:
time: 860 us; the launch traced here: 858 us
  waiting for transfers between devices  411 us (48%)
  blocking collectives  188 us (22%)
  matrix products  111 us (13%)
  other arithmetic  76.3 us (9%)
  local copies, waits for them, and re-layouts  55.4 us (6%)
  between operations  14.5 us (2%)
    all_gather x1, waiting for transfers between devices, body(): piece_values = lax.all_gather(values_flat, 'seq', axis=0, tiled=True)  152 us
    all_gather x1, blocking collectives, body(): piece_tags = lax.all_gather(key_tags, 'seq', axis=0, tiled=True)  149 us
    all_gather x1, waiting for transfers between devices, body(): lax.all_gather(key_matrix, 'seq', axis=0, tiled=True)  114 us
    all_gather x1, waiting for transfers between devices, body(): piece_keys = lax.all_gather(flat_keys, 'seq', axis=0, tiled=True)  84.4 us
    dot_general x16, matrix products, key_block(): jnp.einsum('qhgk,khd->qhgd', raw_weights.astype(jnp.bfloat16), values_par...  55.6 us
    reduce_sum x16, other arithmetic, key_block(): new_totals = old_totals * factor + jnp.sum(raw_weights, axis=-1)  51.6 us
    dot_general x16, matrix products, key_block(): jnp.einsum('qhgd,khd->qhgk', query_rows, keys_part, preferred_element_typ...  45.5 us
    all_gather x1, waiting for transfers between devices, body(): lax.all_gather(w_out, 'seq', axis=1, tiled=True)  33.3 us
  transfers between devices with their start and end apart: 8, of which 6 were waited for; matrix products, arithmetic and copies ran while one was open for 26% of the time, Pallas kernels for 0%

profile of v1, /device:TPU:1, one launch (start us, length us, event | category | flops | bytes accessed | tf_op | source)
XLA Modules:
  0.0 858.1 jit_solution(14100263104265946409)
XLA Ops:
  8.3 8.3 psum.7
  24.4 2.0 fusion.37
  27.9 17.1 %all-gather.9.cloned.1.call-done = bf16[256,2048]{1,0:T(8,128)(2,1)} async-done(((bf16[256,512]{1,0:T(8,128)(2,1)}), bf16[256,2048]{1,0:T(8,128)(2,1)}) %all-gather.9.cloned.1.call-update) | async-done | bytes 1048592 | tf_op jit(solution)/shard_map/all_gather | solution.py:84
  45.0 114.0 %all-gather.11.cloned.1.call-done = bf16[2048,256]{1,0:T(8,128)(2,1)} async-done(((bf16[32,256]{1,0:T(8,128)(2,1)}), bf16[2048,256]{1,0:T(8,128)(2,1)}) %all-gather.11.cloned.1.call-update) | async-done | bytes 1048592 | tf_op jit(solution)/shard_map/all_gather | solution.py:87
  159.1 2.1 multiply_reduce_fusion.1
  162.3 30.7 %all_to_all.5 = bf16[64,32,256]{2,1,0:T(8,128)(2,1)S(1)} all-to-all(bf16[64,32,256]{2,1,0:T(8,128)(2,1)S(1)} %stack.2), channel_id=1, replica_groups=mesh['seq'=64,'mdl'=4] {'seq'}, dimensions={0} | all-to-all | bytes 2097152 | tf_op jit(solution)/shard_map/all_to_all | solution.py:18
  195.6 148.8 %all-gather = bf16[64,1,256]{2,1,0:T(2,128)(2,1)S(1)} all-gather(bf16[1,1,256]{2,1,0:T(2,128)(2,1)S(1)} %reshape.293), channel_id=1, replica_groups=mesh['seq'=64,'mdl'=4] {'seq'}, dimensions={0}, use_global_device_ids=true | all-gather | bytes 33280 | tf_op jit(solution)/shard_map/all_gather | solution.py:146
  344.7 2.3 fusion.42
  348.7 84.4 %all-gather.13.cloned.1.call-done = bf16[16384,256]{1,0:T(8,128)(2,1)} async-done(((bf16[256,256]{1,0:T(8,128)(2,1)}), bf16[16384,256]{1,0:T(8,128)(2,1)}) %all-gather.13.cloned.1.call-update) | async-done | bytes 8388624 | tf_op jit(solution)/shard_map/all_gather | solution.py:144
  433.1 151.5 %all-gather.17.cloned.1.call-done = bf16[16384,256]{1,0:T(8,128)(2,1)} async-done(((bf16[256,256]{1,0:T(8,128)(2,1)}), bf16[16384,256]{1,0:T(8,128)(2,1)}) %all-gather.17.cloned.1.call-update) | async-done | bytes 8388624 | tf_op jit(solution)/shard_map/all_gather | solution.py:145
  584.6 202.4 %while.18 = (s32[]{:T(128)}, f32[256,2,2]{0,2,1:T(2,128)S(1)}, f32[256,2,2]{0,2,1:T(2,128)S(1)}, f32[256,2,2,128]{0,3,2,1:T(8,128)}, s32[16384]{0:T(1024)S(1)}, ...) while((s32[]{:T(128)}, f32[256,2,2]{0,2,1:T(2,128)S(1)}, ...), condition=%wide.region_11.12_spmd.clone, body=%wide.region_8.11_spmd.clone.sunk | while | flops 552737024 | bytes 24471832 | solution.py:183
  586.6 2.8 fusion.68
  589.5 3.2 fusion.70
  592.9 3.5 fusion.72
  599.2 2.8 fusion.68
  602.1 3.2 fusion.70
  605.6 3.5 fusion.72
  611.9 2.8 fusion.68
  614.7 3.2 fusion.70
  618.2 3.5 fusion.72
  624.5 2.8 fusion.68
  627.4 3.2 fusion.70
  630.9 3.5 fusion.72
  637.2 2.8 fusion.68
  640.0 3.2 fusion.70
  643.5 3.5 fusion.72
  649.8 2.8 fusion.68
  652.7 3.2 fusion.70
  656.1 3.5 fusion.72
  662.5 2.8 fusion.68
  665.3 3.2 fusion.70
  668.8 3.5 fusion.72
  675.1 2.8 fusion.68
  678.0 3.2 fusion.70
  681.4 3.5 fusion.72
  687.8 2.8 fusion.68
  690.6 3.2 fusion.70
  694.1 3.5 fusion.72
  700.4 2.8 fusion.68
  703.3 3.2 fusion.70
  706.8 3.5 fusion.72
  713.1 2.8 fusion.68
  715.9 3.2 fusion.70
  719.4 3.5 fusion.72
  725.7 2.8 fusion.68
  728.6 3.2 fusion.70
  732.1 3.5 fusion.72
  738.4 2.8 fusion.68
  741.2 3.2 fusion.70
  744.7 3.5 fusion.72
  751.0 2.8 fusion.68
  753.9 3.2 fusion.70
  757.3 3.5 fusion.72
  763.7 2.8 fusion.68
  766.5 3.2 fusion.70
  770.0 3.5 fusion.72
  776.3 2.8 fusion.68
  779.2 3.2 fusion.70
  782.6 3.5 fusion.72
  788.3 33.3 %all-gather.21.cloned.1.call-done = bf16[512,2048]{0,1:T(8,128)(2,1)} async-done(((bf16[512,32]{0,1:T(8,128)(2,1)}), bf16[512,2048]{0,1:T(8,128)(2,1)}) %all-gather.21.cloned.1.call-update) | async-done | bytes 2097168 | tf_op jit(solution)/shard_map/all_gather | solution.py:207
  821.6 4.6 convolution_convert_fusion
  828.2 6.0 gather_fusion
  834.3 6.0 gather_fusion.1
  841.3 8.3 reduce-scatter.2.cloned.1.call-done
  (305 shorter events, 70.3 us)
Async XLA Ops:
  7.2 154.0 %copy-start.7 = (f32[128]{0:T(128)S(1)}, f32[128]{0:T(128)}, u32[]{:S(2)}) copy-start(f32[128]{0:T(128)} %param.25) | copy-start | bytes 1540
  7.2 155.0 %copy-start.4 = (bf16[32,256]{1,0:T(8,128)(2,1)S(1)}, bf16[32,256]{1,0:T(8,128)(2,1)}, u32[]{:S(2)}) copy-start(bf16[32,256]{1,0:T(8,128)(2,1)} %param.22) | copy-start | bytes 49156
  7.2 37.8 %all-gather.9.cloned.1.call-start = ((), (), s32[]{:S(2)}) async-start(), calls=%async_computation.2 | async-start | bytes 1310720 | tf_op jit(solution)/shard_map/all_gather | solution.py:84
  19.1 140.0 %all-gather.11.cloned.1.call-start = ((), (), s32[]{:S(2)}) async-start(), calls=%async_computation.3 | async-start | bytes 1064960 | tf_op jit(solution)/shard_map/all_gather | solution.py:87
  19.8 324.8 %all-gather.15.cloned.1.call-start = ((), (), s32[]{:S(2)}) async-start(), calls=%async_computation.5 | async-start | bytes 2129920 | tf_op jit(solution)/shard_map/all_gather | solution.py:86
  20.6 412.5 %all-gather.13.cloned.1.call-start = ((), (), s32[]{:S(2)}) async-start(), calls=%async_computation.4 | async-start | bytes 8519680 | tf_op jit(solution)/shard_map/all_gather | solution.py:144
  45.0 148.0 %copy-start = (bf16[256,2048]{1,0:T(8,128)(2,1)S(1)}, bf16[256,2048]{1,0:T(8,128)(2,1)}, u32[]{:S(2)}) copy-start(bf16[256,2048]{1,0:T(8,128)(2,1)} %all-gather.9.cloned.1.call-done) | copy-start | bytes 3145732
  161.1 34.4 %copy-start.5 = (s32[256]{0:T(256)S(1)}, s32[256]{0:T(256)}, u32[]{:S(2)}) copy-start(s32[256]{0:T(256)} %param.28) | copy-start | bytes 3076
  161.2 34.4 %copy-start.6 = (s32[256]{0:T(256)S(1)}, s32[256]{0:T(256)}, u32[]{:S(2)}) copy-start(s32[256]{0:T(256)} %param.30) | copy-start | bytes 3076
  162.1 422.4 %all-gather.17.cloned.1.call-start = ((), (), s32[]{:S(2)}) async-start(), calls=%async_computation.6 | async-start | bytes 8519680 | tf_op jit(solution)/shard_map/all_gather | solution.py:145
  193.0 154.5 %copy-start.8 = (f32[128]{0:T(128)S(1)}, f32[128]{0:T(128)}, u32[]{:S(2)}) copy-start(f32[128]{0:T(128)} %param.24) | copy-start | bytes 1540
  194.2 594.1 %all-gather.19.cloned.1.call-start = ((), (), s32[]{:S(2)}) async-start(), calls=%async_computation.7 | async-start | bytes 2129920 | tf_op jit(solution)/shard_map/all_gather | solution.py:89
  194.7 626.9 %all-gather.21.cloned.1.call-start = ((), (), s32[]{:S(2)}) async-start(), calls=%async_computation.8 | async-start | bytes 2129920 | tf_op jit(solution)/shard_map/all_gather | solution.py:207
  195.5 654.1 %reduce-scatter.2.cloned.1.call-start = ((), (), s32[]{:S(2)}) async-start(), calls=%async_computation.9 | async-start | bytes 1310720 | tf_op jit(solution)/shard_map/reduce_scatter | solution.py:210
  586.6 6.3 copy-start.2
  596.4 0.8 copy-start.3
  599.2 6.3 copy-start.2
  609.1 0.8 copy-start.3
  611.9 6.3 copy-start.2
  621.7 0.8 copy-start.3
  624.5 6.3 copy-start.2
  634.3 0.8 copy-start.3
  637.2 6.3 copy-start.2
  647.0 0.8 copy-start.3
  649.8 6.3 copy-start.2
  659.6 0.8 copy-start.3
  662.5 6.3 copy-start.2
  672.3 0.8 copy-start.3
  675.1 6.3 copy-start.2
  684.9 0.8 copy-start.3
  687.8 6.3 copy-start.2
  697.6 0.8 copy-start.3
  700.4 6.3 copy-start.2
  710.2 0.8 copy-start.3
  713.1 6.3 copy-start.2
  722.9 0.8 copy-start.3
  725.7 6.3 copy-start.2
  735.5 0.8 copy-start.3
  738.4 6.3 copy-start.2
  748.2 0.8 copy-start.3
  751.0 6.3 copy-start.2
  760.8 0.8 copy-start.3
  763.6 6.3 copy-start.2
  773.5 0.8 copy-start.3
  776.3 6.3 copy-start.2
  786.1 0.8 copy-start.3
  826.2 23.4 %copy-start.1 = (bf16[256,512]{1,0:T(8,128)(2,1)S(1)}, bf16[256,512]{1,0:T(8,128)(2,1)}, u32[]{:S(2)}) copy-start(bf16[256,512]{1,0:T(8,128)(2,1)} %param.18) | copy-start | bytes 786436
Sparse Core Ops, SparseCore 0:
  19.2 25.7 all-gather.8
  48.6 110.3 all-gather.10
  162.7 117.9 all-gather.14
  284.6 148.4 all-gather.12
  437.0 147.5 all-gather.16
  588.0 114.5 all-gather.18
  706.2 115.3 all-gather.20
  826.4 23.1 reduce-scatter.1
